TPU v7x, 256 devices: a whole 4x4x8 slice. The times are simulated.
256 devices in a mesh: dp: 64 (over y, z, core), tensor: 4 (over x).
Axes of the slice: x: 4, y: 4, z: 8, core: 2. Of those that a mesh axis runs over, the one named last changes fastest.
Arguments:
- activations: bfloat16 [32768, 8192], P('dp', 'tensor'), may hold values from -2000 to 2000
- norm_gain: float32 [8192], replicated, may hold values from 0.5 to 12
- w_query: bfloat16 [8192, 4096], P('dp', 'tensor'), may hold values from -0.0625 to 0.0625
- w_key: bfloat16 [8192, 512], P('dp', 'tensor'), may hold values from -0.0625 to 0.0625
- w_value: bfloat16 [8192, 512], P('dp', 'tensor'), may hold values from -0.0625 to 0.0625
- lengths: int32 [128], replicated, may hold values from 128 to 256
- languages: int32 [128], replicated, may hold values from 0 to 29
- lang_caps: int32 [30], replicated, may hold values from 128 to 256
- dest_shard: int32 [128], replicated, may hold values from 0 to 63, as said below
Outputs:
- attended: bfloat16 [32768, 4096], P('dp', 'tensor')
Inputs may be any that keep to these rules, and one draw needn't show every extreme that they name: `dest_shard`: every data shard receives exactly 2 documents.
All inputs are finite; a program needn't handle non-finite values.
Results may differ from a plain program's by a relative error of at most 0.007.
The roundings to bfloat16 on the way count: a program that leaves them out, or rounds other values in their place, can miss the bound.
Values may be sent and summed in bfloat16 or wider, within the bound.
A program may use at most 128 MiB of HBM per device.

v0:
```python
import math

import jax
import jax.numpy as jnp
from jax import lax
from jax.sharding import PartitionSpec as P

HEAD_WIDTH = 128


rope_base = 500000.0
norm_eps = 1e-05


def rotary_embedding(vectors, token_positions):
    half_width = vectors.shape[-1] // 2
    steps_range = jnp.arange(half_width, dtype=jnp.float32)
    frequency = jnp.exp(steps_range * (-2.0 * math.log(rope_base) / vectors.shape[-1]))
    angles = token_positions[..., None, None] * frequency
    cosine = jnp.cos(angles)
    sine_table = jnp.sin(angles)
    first_half = vectors[..., :half_width]
    second_half = vectors[..., half_width:]
    return jnp.concatenate(
        [
            first_half * cosine - second_half * sine_table,
            second_half * cosine + first_half * sine_table,
        ],
        axis=-1,
    )


def project(source_rows, norm_gain, w_query, w_key, w_value):
    gathered = lax.all_gather(source_rows, "tensor", axis=1, tiled=True)
    widened = gathered.astype(jnp.float32)
    row_scale = lax.rsqrt(jnp.mean(widened * widened, axis=1, keepdims=True) + norm_eps)
    normed = (widened * row_scale * norm_gain).astype(jnp.bfloat16)
    pieces = (
        lax.all_gather(w_query, "dp", axis=0, tiled=True),
        lax.all_gather(w_key, "dp", axis=0, tiled=True),
        lax.all_gather(w_value, "dp", axis=0, tiled=True),
    )
    return tuple(
        (
            jnp.dot(normed, weight_piece, preferred_element_type=jnp.float32)
            for weight_piece in pieces
        )
    )


def rotate_round(query_part, key_portion, value_portion, token_positions, head_dim):
    total_rows = query_part.shape[0]
    rotated_query = rotary_embedding(
        query_part.reshape(total_rows, -1, head_dim), token_positions
    ).reshape(total_rows, -1)
    rotated_key = rotary_embedding(
        key_portion.reshape(total_rows, -1, head_dim), token_positions
    ).reshape(total_rows, -1)
    return jnp.concatenate([rotated_query, rotated_key, value_portion], axis=1).astype(jnp.bfloat16)


def attend(packed, doc_lengths, query_width, key_width, head_dim, doc_max):
    total_rows = packed.shape[0]
    doc_total = total_rows // doc_max
    value_head_rows = key_width // head_dim
    heads_per_group = query_width // key_width
    queries = packed[:, :query_width].reshape(
        doc_total, doc_max, value_head_rows, heads_per_group, head_dim
    )
    key_rows = packed[:, query_width : query_width + key_width].reshape(
        doc_total, doc_max, value_head_rows, head_dim
    )
    value_rows = packed[:, query_width + key_width :].reshape(
        doc_total, doc_max, value_head_rows, head_dim
    )
    scores = jnp.einsum(
        "jqhgd,jkhd->jhgqk", queries, key_rows, preferred_element_type=jnp.float32
    ) / math.sqrt(head_dim)
    order_range = jnp.arange(doc_max)
    causal = order_range[:, None] >= order_range[None, :]
    scores = jnp.where(causal, scores, -jnp.inf)
    row_peak = jnp.max(scores, axis=-1, keepdims=True)
    exponent = jnp.exp(scores - row_peak)
    probability = (exponent / jnp.sum(exponent, axis=-1, keepdims=True)).astype(jnp.bfloat16)
    blended = jnp.einsum(
        "jhgqk,jkhd->jqhgd", probability, value_rows, preferred_element_type=jnp.float32
    )
    blended = blended.reshape(doc_total, doc_max, query_width)
    row_valid = order_range[None, :] < doc_lengths[:, None]
    result = jnp.where(row_valid[..., None], blended, 0.0)
    return result.reshape(total_rows, query_width).astype(jnp.bfloat16)


def local(
    activations, norm_gain, w_query, w_key, w_value, lengths, languages, lang_caps, dest_shard
):
    shard_count = lax.axis_size("dp")
    my_shard = lax.axis_index("dp")
    doc_count = lengths.shape[0]
    token_rows = activations.shape[0]
    rows_peer = token_rows // doc_count
    doc_max = rows_peer * shard_count
    docs_here = doc_count // shard_count
    head_dim = HEAD_WIDTH
    query_width = w_query.shape[1]
    key_width = w_key.shape[1]
    language_table = jnp.arange(lang_caps.shape[0])
    cap_of_doc = jnp.sum(
        jnp.where(languages[:, None] == language_table[None, :], lang_caps[None, :], 0), axis=1
    )
    capped = jnp.minimum(lengths, cap_of_doc)
    doc_order = jnp.arange(doc_count)
    same_dest = dest_shard[:, None] == dest_shard[None, :]
    doc_rank = jnp.sum(
        (same_dest & (doc_order[None, :] < doc_order[:, None])).astype(jnp.int32), axis=1
    )
    target_slot = dest_shard * docs_here + doc_rank
    holder = jnp.sum(
        jnp.where(doc_order[:, None] == target_slot[None, :], doc_order[None, :], 0), axis=1
    )
    mine = lax.dynamic_slice_in_dim(holder, my_shard * docs_here, docs_here)
    doc_lengths = jnp.take(capped, mine)
    holder_grid = jnp.transpose(holder.reshape(shard_count, docs_here))
    send_index = (
        holder_grid[:, None, :] * rows_peer + jnp.arange(rows_peer)[None, :, None]
    ).reshape(-1)
    outgoing = jnp.take(activations, send_index, axis=0).reshape(
        docs_here, rows_peer, shard_count, -1
    )
    arrived = lax.all_to_all(outgoing, "dp", split_axis=2, concat_axis=2, tiled=True)
    moved_rows = arrived.reshape(docs_here * doc_max, -1)
    query_part, key_portion, value_portion = project(moved_rows, norm_gain, w_query, w_key, w_value)
    token_positions = jnp.tile(jnp.arange(doc_max), docs_here).astype(jnp.float32)
    packed = rotate_round(query_part, key_portion, value_portion, token_positions, head_dim)
    return attend(packed, doc_lengths, query_width, key_width, head_dim, doc_max)


def solution(mesh):
    return jax.shard_map(
        local,
        mesh=mesh,
        in_specs=(
            P("dp", "tensor"),
            P(),
            P("dp", "tensor"),
            P("dp", "tensor"),
            P("dp", "tensor"),
            P(),
            P(),
            P(),
            P(),
        ),
        out_specs=P("dp", "tensor"),
        check_vma=False,
    )
```

profile of v0, /device:TPU:1, one launch (start us, length us, event | category | flops | bytes accessed | tf_op | source)
XLA Modules:
  0.0 453.7 jit_solution(18384676850716704676)
XLA Ops:
  6.5 0.0 copy-start
  6.5 0.0 all-gather.5.cloned.1.call-start
  6.5 1.0 convert_reduce_fusion
  7.5 0.7 multiply_add_fusion
  8.2 0.1 select_reduce_fusion
  8.3 0.1 mul.188
  8.5 0.1 copy.35
  8.6 0.1 add.84
  8.7 0.1 copy.36
  8.8 0.0 copy-done
  8.8 3.3 gather_fusion.1
  12.2 3.8 copy_select_fusion
  16.0 64.1 %all_to_all.5 = bf16[2,4,64,2048]{3,1,0,2:T(4,128)(2,1)S(1)} all-to-all(bf16[2,4,64,2048]{3,1,0,2:T(4,128)(2,1)S(1)} %copy_select_fusion), channel_id=1, replica_groups=mesh['dp'=64,'tensor'=4] {'dp'}, dimensions={2} | all-to-all | bytes 4194304 | tf_op jit(solution)/shard_map/all_to_all | solution.py:130
  80.1 2.5 copy.38
  82.7 0.0 all-gather.5.cloned.1.call-update
  82.7 0.0 all-gather.9.cloned.1.call-start
  82.7 0.7 all-gather.9.cloned.1.call-update
  83.4 0.0 all-gather.7.cloned.1.call-start
  83.5 0.7 all-gather.7.cloned.1.call-update
  84.2 0.0 all-gather.11.cloned.1.call-start
  84.2 0.5 all-gather.11.cloned.1.call-update
  84.8 0.0 copy-done.2
  84.8 0.0 copy-done.3
  84.8 0.1 select_reduce_fusion.1
  84.9 0.1 compare_select_fusion.2
  85.0 0.6 gather_fusion
  85.6 0.1 and_select_fusion
  85.7 0.1 iota_compare_fusion.4
  85.8 1.0 multiply_cosine_fusion
  86.8 0.0 copy-start.1
  86.8 77.9 %all-gather.5.cloned.1.call-done = bf16[512,8192]{1,0:T(8,128)(2,1)} async-done(((bf16[512,2048]{1,0:T(8,128)(2,1)}), bf16[512,8192]{1,0:T(8,128)(2,1)}) %all-gather.5.cloned.1.call-update) | async-done | bytes 8388624 | tf_op jit(solution)/shard_map/all_gather | solution.py:34
  164.7 5.1 %fusion = f32[512]{0:T(512)S(1)} fusion(bf16[512,8192]{1,0:T(8,128)(2,1)} %all-gather.5.cloned.1.call-done), kind=kLoop, calls=%fused_computation.4 | loop fusion | flops 12582400 | bytes 8390656 | tf_op jit(solution)/shard_map/reduce_sum | solution.py:36
  169.8 76.8 %all-gather.9.cloned.1.call-done = bf16[8192,128]{1,0:T(8,128)(2,1)} async-done(((bf16[128,128]{1,0:T(8,128)(2,1)}), bf16[8192,128]{1,0:T(8,128)(2,1)}) %all-gather.9.cloned.1.call-update) | async-done | bytes 2097168 | tf_op jit(solution)/shard_map/all_gather | solution.py:40
  246.6 6.5 %convolution_bitcast_fusion.1 = f32[512,1,128]{0,2,1:T(8,128)S(1)} fusion(bf16[8192,128]{1,0:T(8,128)(2,1)} %all-gather.9.cloned.1.call-done, bf16[512,8192]{1,0:T(8,128)(2,1)} %all-gather.5.cloned.1.call-done, f32[8192]{0:T(1024)S(1)} %copy-done.1, f32[512]{0:T(512)S(1)} %add_rsqrt_fusion), kind=kOutput, calls=%fused_computation.22 | convolution fusion | flops 1090519040 | bytes 10782720 | tf_op jit(solution)/shard_map/dot_general | solution.py:45
  253.1 0.6 fusion.19
  253.7 0.1 copy.49
  253.8 70.6 %all-gather.7.cloned.1.call-done = bf16[8192,128]{1,0:T(8,128)(2,1)} async-done(((bf16[128,128]{1,0:T(8,128)(2,1)}), bf16[8192,128]{1,0:T(8,128)(2,1)}) %all-gather.7.cloned.1.call-update) | async-done | bytes 2097168 | tf_op jit(solution)/shard_map/all_gather | solution.py:41
  324.4 6.4 %convolution_convert_fusion = bf16[512,128]{1,0:T(8,128)(2,1)S(1)} fusion(bf16[8192,128]{1,0:T(8,128)(2,1)} %all-gather.7.cloned.1.call-done, bf16[512,8192]{1,0:T(8,128)(2,1)} %all-gather.5.cloned.1.call-done, f32[8192]{0:T(1024)S(1)} %copy-done.1, f32[512]{0:T(512)S(1)} %add_rsqrt_fusion), kind=kOutput, calls=%fused_computation.23 | convolution fusion | flops 1090584576 | bytes 10651648 | tf_op jit(solution)/shard_map/dot_general | solution.py:45
  330.8 93.0 %all-gather.11.cloned.1.call-done = bf16[8192,1024]{1,0:T(8,128)(2,1)} async-done(((bf16[128,1024]{1,0:T(8,128)(2,1)}), bf16[8192,1024]{1,0:T(8,128)(2,1)}) %all-gather.11.cloned.1.call-update) | async-done | bytes 16777232 | tf_op jit(solution)/shard_map/all_gather | solution.py:39
  423.8 14.5 %convolution_bitcast_fusion = f32[64,8,8,128]{3,1,2,0:T(8,128)S(1)} fusion(bf16[8192,1024]{1,0:T(8,128)(2,1)} %all-gather.11.cloned.1.call-done, bf16[512,8192]{1,0:T(8,128)(2,1)} %all-gather.5.cloned.1.call-done, f32[8192]{0:T(1024)S(1)} %copy-done.1, f32[512]{0:T(512)S(1)} %add_rsqrt_fusion), kind=kOutput, calls=%fused_computation.21 | convolution fusion | flops 8606711808 | bytes 27297792 | tf_op jit(solution)/shard_map/dot_general | solution.py:45
  438.3 0.5 copy.51
  438.8 0.9 subtract_convert_fusion
  439.7 0.6 pad_maximum_fusion
  440.3 0.8 fusion.4
  441.0 0.9 fusion.3
  441.9 2.3 fusion.9
  444.2 1.7 copy.43
  445.9 1.2 fusion.5
  (19 shorter events, 0.2 us)
Async XLA Ops:
  6.5 2.3 copy-start
  6.5 158.2 %all-gather.5.cloned.1.call-start = ((), (), s32[]{:S(2)}) async-start(), calls=%async_computation.1 | async-start | bytes 10485760 | tf_op jit(solution)/shard_map/all_gather | solution.py:34
  80.1 4.6 %copy-start.2 = (s32[30]{0:T(128)S(1)}, s32[30]{0:T(128)}, u32[]{:S(2)}) copy-start(s32[30]{0:T(128)} %param.16) | copy-start | bytes 364
  80.1 4.6 %copy-start.3 = (s32[128]{0:T(128)S(1)}, s32[128]{0:T(128)}, u32[]{:S(2)}) copy-start(s32[128]{0:T(128)} %param.15) | copy-start | bytes 1540
  80.1 4.7 %copy-start.4 = (s32[128]{0:T(128)S(1)}, s32[128]{0:T(128)}, u32[]{:S(2)}) copy-start(s32[128]{0:T(128)} %param.14) | copy-start | bytes 1540
  82.7 164.0 %all-gather.9.cloned.1.call-start = ((), (), s32[]{:S(2)}) async-start(), calls=%async_computation.3 | async-start | bytes 2129920 | tf_op jit(solution)/shard_map/all_gather | solution.py:40
  83.4 241.0 %all-gather.7.cloned.1.call-start = ((), (), s32[]{:S(2)}) async-start(), calls=%async_computation.2 | async-start | bytes 2129920 | tf_op jit(solution)/shard_map/all_gather | solution.py:41
  84.2 339.6 %all-gather.11.cloned.1.call-start = ((), (), s32[]{:S(2)}) async-start(), calls=%async_computation.4 | async-start | bytes 17039360 | tf_op jit(solution)/shard_map/all_gather | solution.py:39
  86.8 159.8 %copy-start.1 = (f32[8192]{0:T(1024)S(1)}, f32[8192]{0:T(1024)}, u32[]{:S(2)}) copy-start(f32[8192]{0:T(1024)} %param.10) | copy-start | bytes 98308
Sparse Core Ops, SparseCore 0:
  82.8 81.8 all-gather.4
  167.5 79.0 all-gather.8
  249.4 74.9 all-gather.6
  327.1 96.6 all-gather.10
where the time goes:
time: 454 us
  waiting for transfers between devices  320 us (70%)
  blocking collectives  64.1 us (14%)
  matrix products  30.4 us (7%)
  other arithmetic  16.2 us (4%)
  between operations  13.3 us (3%)
  local copies, waits for them, and re-layouts  9.25 us (2%)
    all_gather x1, waiting for transfers between devices, project(): lax.all_gather(w_query, 'dp', axis=0, tiled=True)  93 us
    all_gather x1, waiting for transfers between devices, project(): gathered = lax.all_gather(source_rows, 'tensor', axis=1, tiled=True)  77.9 us
    all_gather x1, waiting for transfers between devices, project(): lax.all_gather(w_key, 'dp', axis=0, tiled=True)  76.8 us
    all_gather x1, waiting for transfers between devices, project(): lax.all_gather(w_value, 'dp', axis=0, tiled=True)  70.6 us
    all_to_all x1, blocking collectives, local(): lax.all_to_all(outgoing, 'dp', split_axis=2, concat_axis=2, tiled=True)  64.1 us
    dot_general x3, matrix products, project(): jnp.dot(normed, weight_piece, preferred_element_type=jnp.float32)  27.4 us
  transfers between devices with their start and end apart: 4, of which 4 were waited for; matrix products, arithmetic and copies ran while one was open for 5% of the time, Pallas kernels for 0%

commit v1 on v0

--- a/solution.py
+++ b/solution.py
@@ -31,32 +31,21 @@
 
 
 def project(source_rows, norm_gain, w_query, w_key, w_value):
+    packed_weight = jnp.concatenate([w_query, w_key, w_value], axis=1)
+    weight = lax.all_gather(packed_weight, "dp", axis=0, tiled=True)
     gathered = lax.all_gather(source_rows, "tensor", axis=1, tiled=True)
     widened = gathered.astype(jnp.float32)
     row_scale = lax.rsqrt(jnp.mean(widened * widened, axis=1, keepdims=True) + norm_eps)
     normed = (widened * row_scale * norm_gain).astype(jnp.bfloat16)
-    pieces = (
-        lax.all_gather(w_query, "dp", axis=0, tiled=True),
-        lax.all_gather(w_key, "dp", axis=0, tiled=True),
-        lax.all_gather(w_value, "dp", axis=0, tiled=True),
-    )
-    return tuple(
-        (
-            jnp.dot(normed, weight_piece, preferred_element_type=jnp.float32)
-            for weight_piece in pieces
-        )
-    )
+    return jnp.dot(normed, weight, preferred_element_type=jnp.float32)
 
 
-def rotate_round(query_part, key_portion, value_portion, token_positions, head_dim):
-    total_rows = query_part.shape[0]
-    rotated_query = rotary_embedding(
-        query_part.reshape(total_rows, -1, head_dim), token_positions
+def rotate_round(projected, token_positions, rotated_width, head_dim):
+    total_rows = projected.shape[0]
+    rotated = rotary_embedding(
+        projected[:, :rotated_width].reshape(total_rows, -1, head_dim), token_positions
     ).reshape(total_rows, -1)
-    rotated_key = rotary_embedding(
-        key_portion.reshape(total_rows, -1, head_dim), token_positions
-    ).reshape(total_rows, -1)
-    return jnp.concatenate([rotated_query, rotated_key, value_portion], axis=1).astype(jnp.bfloat16)
+    return jnp.concatenate([rotated, projected[:, rotated_width:]], axis=1).astype(jnp.bfloat16)
 
 
 def attend(packed, doc_lengths, query_width, key_width, head_dim, doc_max):
@@ -124,15 +113,17 @@
     send_index = (
         holder_grid[:, None, :] * rows_peer + jnp.arange(rows_peer)[None, :, None]
     ).reshape(-1)
-    outgoing = jnp.take(activations, send_index, axis=0).reshape(
+    token_positions = (
+        my_shard + shard_count * (jnp.arange(token_rows) % rows_peer)
+    ).astype(jnp.float32)
+    projected = project(activations, norm_gain, w_query, w_key, w_value)
+    packed = rotate_round(projected, token_positions, query_width + key_width, head_dim)
+    outgoing = jnp.take(packed, send_index, axis=0, mode="clip").reshape(
         docs_here, rows_peer, shard_count, -1
     )
     arrived = lax.all_to_all(outgoing, "dp", split_axis=2, concat_axis=2, tiled=True)
     moved_rows = arrived.reshape(docs_here * doc_max, -1)
-    query_part, key_portion, value_portion = project(moved_rows, norm_gain, w_query, w_key, w_value)
-    token_positions = jnp.tile(jnp.arange(doc_max), docs_here).astype(jnp.float32)
-    packed = rotate_round(query_part, key_portion, value_portion, token_positions, head_dim)
-    return attend(packed, doc_lengths, query_width, key_width, head_dim, doc_max)
+    return attend(moved_rows, doc_lengths, query_width, key_width, head_dim, doc_max)
 
 
 def solution(mesh):

time: 454 us -> 293 us (0.65)
  waiting for transfers between devices: 320 us -> 231 us
  blocking collectives: 64.1 us -> 0 us
  matrix products: 30.4 us -> 18.6 us
  starting transfers between devices: 0.12 us -> 6.01 us
    all_gather x3 -> x1, waiting for transfers between devices: 240 us -> 109 us  [project(): weight = lax.all_gather(packed_weight, 'dp', axis=0, tiled=True)]
    all_to_all x1 -> x0, blocking collectives: 64.1 us -> none  [local(): lax.all_to_all(outgoing, 'dp', split_axis=2, concat_axis=2, tiled=True)]
    all_to_all x0 -> x1, waiting for transfers between devices: none -> 33.1 us  [local(): lax.all_to_all(outgoing, 'dp', split_axis=2, concat_axis=2, tiled=True)]
    dot_general x3 -> x1, matrix products: 27.4 us -> 16.5 us  [project(): return jnp.dot(normed, weight, preferred_element_type=jnp.float32)]
    all_gather x1, waiting for transfers between devices: 77.9 us -> 88.1 us  [project(): gathered = lax.all_gather(source_rows, 'tensor', axis=1, tiled=True)]
    all_to_all x0 -> x1, starting transfers between devices: none -> 5.97 us  [local(): lax.all_to_all(outgoing, 'dp', split_axis=2, concat_axis=2, tiled=True)]
  transfers between devices with their start and end apart: 4 -> 3, of which waited for: 4 -> 3; matrix products, arithmetic and copies ran while one was open for 5% -> 3% of each run, Pallas kernels for 0% -> 0%
where the time goes in v1:
time: 293 us
  waiting for transfers between devices  231 us (79%)
  matrix products  18.6 us (6%)
  between operations  13.6 us (5%)
  other arithmetic  12 us (4%)
  local copies, waits for them, and re-layouts  11.6 us (4%)
  starting transfers between devices  6.01 us (2%)
    all_gather x1, waiting for transfers between devices, project(): weight = lax.all_gather(packed_weight, 'dp', axis=0, tiled=True)  109 us
    all_gather x1, waiting for transfers between devices, project(): gathered = lax.all_gather(source_rows, 'tensor', axis=1, tiled=True)  88.1 us
    all_to_all x1, waiting for transfers between devices, local(): lax.all_to_all(outgoing, 'dp', split_axis=2, concat_axis=2, tiled=True)  33.1 us
    dot_general x1, matrix products, project(): return jnp.dot(normed, weight, preferred_element_type=jnp.float32)  16.5 us
    all_to_all x1, starting transfers between devices, local(): lax.all_to_all(outgoing, 'dp', split_axis=2, concat_axis=2, tiled=True)  5.97 us
  transfers between devices with their start and end apart: 3, of which 3 were waited for; matrix products, arithmetic and copies ran while one was open for 3% of the time, Pallas kernels for 0%

profile of v1, /device:TPU:1, one launch (start us, length us, event | category | flops | bytes accessed | tf_op | source)
XLA Modules:
  0.0 293.0 jit_solution(14304292000981293359)
XLA Ops:
  6.5 0.0 copy-start.1
  6.5 0.0 all-gather.3.cloned.1.call-start
  6.5 0.7 all-gather.3.cloned.1.call-update
  7.3 0.0 all-gather.5.cloned.1.call-start
  7.3 1.7 pad_maximum_fusion.2
  9.0 0.0 all-gather.5.cloned.1.call-update
  9.1 0.0 copy-done.1
  9.1 0.2 convert_reduce_fusion
  9.3 0.1 select_reduce_fusion
  9.4 0.1 mul.133
  9.5 0.1 copy.30
  9.6 0.1 reshape.215
  9.7 0.5 multiply_cosine_fusion
  10.3 0.0 copy-start
  10.3 88.1 %all-gather.3.cloned.1.call-done = bf16[512,8192]{1,0:T(8,128)(2,1)} async-done(((bf16[512,2048]{1,0:T(8,128)(2,1)}), bf16[512,8192]{1,0:T(8,128)(2,1)}) %all-gather.3.cloned.1.call-update) | async-done | bytes 8388624 | tf_op jit(solution)/shard_map/all_gather | solution.py:36
  98.4 5.1 %fusion = f32[512]{0:T(512)S(1)} fusion(bf16[512,8192]{1,0:T(8,128)(2,1)} %all-gather.3.cloned.1.call-done), kind=kLoop, calls=%fused_computation.4 | loop fusion | flops 12582400 | bytes 8390656 | tf_op jit(solution)/shard_map/reduce_sum | solution.py:38
  103.5 109.2 %all-gather.5.cloned.1.call-done = bf16[8192,1280]{1,0:T(8,128)(2,1)} async-done(((bf16[128,1280]{1,0:T(8,128)(2,1)}), bf16[8192,1280]{1,0:T(8,128)(2,1)}) %all-gather.5.cloned.1.call-update) | async-done | bytes 20971536 | tf_op jit(solution)/shard_map/all_gather | solution.py:35
  212.7 0.0 copy-done
  212.7 16.5 %fusion.3 = f32[512,1280]{1,0:T(8,128)S(1)} fusion(bf16[8192,1280]{1,0:T(8,128)(2,1)} %all-gather.5.cloned.1.call-done, bf16[512,8192]{1,0:T(8,128)(2,1)} %all-gather.3.cloned.1.call-done, f32[8192]{0:T(1024)S(1)} %copy-done, f32[512]{0:T(512)S(1)} %add_rsqrt_fusion), kind=kOutput, calls=%fused_computation.7 | convolution fusion | flops 10754195456 | bytes 32016384 | tf_op jit(solution)/shard_map/dot_general | solution.py:40
  229.3 1.6 slice.33
  230.9 2.0 copy.28
  232.9 0.4 subtract_convert_fusion
  233.3 0.1 pad_maximum_fusion.1
  233.4 1.4 copy.29
  234.8 1.4 pad_maximum_fusion
  236.2 2.1 gather_fusion.1
  238.3 0.0 copy-start.2
  238.3 0.0 copy-start.3
  238.3 0.0 copy-start.4
  238.4 2.1 copy.31
  240.4 6.0 %all-to-all-start = ((bf16[2,4,64,1280]{3,1,0,2:T(4,128)(2,1)}), bf16[2,4,64,1280]{3,1,0,2:T(4,128)(2,1)S(1)}, u32[]{:S(2)}, u32[]{:S(2)}) async-start(bf16[2,4,64,1280]{3,1,0,2:T(4,128)(2,1)} %copy.31), calls=%async_computation | async-start | bytes 2621440 | tf_op jit(solution)/shard_map/all_to_all | solution.py:124
  246.4 0.0 copy-done.2
  246.4 0.0 copy-done.3
  246.4 0.1 select_reduce_fusion.1
  246.5 0.0 copy-done.4
  246.5 0.1 compare_select_fusion
  246.6 0.6 gather_fusion
  247.3 0.1 and_select_fusion
  247.3 0.1 iota_compare_fusion.4
  247.5 33.1 %all-to-all-done = bf16[2,4,64,1280]{3,1,0,2:T(4,128)(2,1)S(1)} async-done(((bf16[2,4,64,1280]{3,1,0,2:T(4,128)(2,1)}), bf16[2,4,64,1280]{3,1,0,2:T(4,128)(2,1)S(1)}, u32[]{:S(2)}, u32[]{:S(2)}) %all-to-all-start) | async-done | bytes 1310752 | tf_op jit(solution)/shard_map/all_to_all | solution.py:124
  280.5 0.2 copy.32
  280.8 0.1 slice_bitcast_fusion
  280.9 0.3 copy.42
  281.2 0.8 fusion.8
  282.0 0.9 fusion.7
  282.9 1.3 fusion.13
  284.2 0.8 copy.36
  284.9 1.2 fusion.9
  (13 shorter events, 0.2 us)
Async XLA Ops:
  6.5 2.5 copy-start.1
  6.5 91.9 %all-gather.3.cloned.1.call-start = ((), (), s32[]{:S(2)}) async-start(), calls=%async_computation.1 | async-start | bytes 10485760 | tf_op jit(solution)/shard_map/all_gather | solution.py:36
  7.3 205.5 %all-gather.5.cloned.1.call-start = ((), (), s32[]{:S(2)}) async-start(), calls=%async_computation.2 | async-start | bytes 21299200 | tf_op jit(solution)/shard_map/all_gather | solution.py:35
  10.3 202.4 %copy-start = (f32[8192]{0:T(1024)S(1)}, f32[8192]{0:T(1024)}, u32[]{:S(2)}) copy-start(f32[8192]{0:T(1024)} %param.10) | copy-start | bytes 98308
  238.3 8.1 %copy-start.2 = (s32[30]{0:T(128)S(1)}, s32[30]{0:T(128)}, u32[]{:S(2)}) copy-start(s32[30]{0:T(128)} %param.16) | copy-start | bytes 364
  238.3 8.1 %copy-start.3 = (s32[128]{0:T(128)S(1)}, s32[128]{0:T(128)}, u32[]{:S(2)}) copy-start(s32[128]{0:T(128)} %param.15) | copy-start | bytes 1540
  238.3 8.2 %copy-start.4 = (s32[128]{0:T(128)S(1)}, s32[128]{0:T(128)}, u32[]{:S(2)}) copy-start(s32[128]{0:T(128)} %param.14) | copy-start | bytes 1540
  240.4 40.1 %all-to-all-start = ((bf16[2,4,64,1280]{3,1,0,2:T(4,128)(2,1)}), bf16[2,4,64,1280]{3,1,0,2:T(4,128)(2,1)S(1)}, u32[]{:S(2)}, u32[]{:S(2)}) async-start(bf16[2,4,64,1280]{3,1,0,2:T(4,128)(2,1)} %copy.31), calls=%async_computation | async-start | bytes 2621440 | tf_op jit(solution)/shard_map/all_to_all | solution.py:124
Sparse Core Ops, SparseCore 0:
  9.1 89.2 all-gather.2
  101.1 111.5 all-gather.4

commit v2 on v1

--- a/solution.py
+++ b/solution.py
@@ -1,8 +1,12 @@
+import functools
+import heapq
 import math
 
 import jax
 import jax.numpy as jnp
 from jax import lax
+from jax.experimental import pallas as pl
+from jax.experimental.pallas import tpu as pltpu
 from jax.sharding import PartitionSpec as P
 
 HEAD_WIDTH = 128
@@ -12,40 +16,304 @@
 norm_eps = 1e-05
 
 
-def rotary_embedding(vectors, token_positions):
-    half_width = vectors.shape[-1] // 2
+MESH = pl.DeviceIdType.MESH
+LANES = 128
+Y_CHIPS, Z_CHIPS, CORES, X_CHIPS = 4, 8, 2, 4
+ROW_CHUNKS = 4
+LEFT_COLUMNS = 768
+
+
+def hops_az(s):
+    return 4 if s == 1 else 3
+
+
+def hops_ay(s, dz):
+    return 2 if (dz % 2 == 0) == (s == 1) else 1
+
+
+def hops_by(s):
+    return 1 if s == 1 else 2
+
+
+def hops_bz(s, dy):
+    return 4 if (dy % 2 == 0) == (s == 1) else 3
+
+
+def first_sends():
+    sends = [("az", s, 1) for s in (1, -1)] + [("by", s, 1) for s in (1, -1)]
+    sends += [("ay", s, 0, 1) for s in (1, -1)] + [("bz", s, 0, 1) for s in (1, -1)]
+    return sends + [("xo", s, r) for r in range(2) for s in (1, -1)]
+
+
+def next_sends(key):
+    kind, s = key[:2]
+    sends = []
+    if kind == "az":
+        if key[2] < hops_az(s):
+            sends.append(("az", s, key[2] + 1))
+        sends += [("ay", q, -s * key[2], 1) for q in (1, -1)]
+    elif kind == "ay":
+        if key[3] < hops_ay(s, key[2]):
+            sends.append(("ay", s, key[2], key[3] + 1))
+    elif kind == "by":
+        if key[2] < hops_by(s):
+            sends.append(("by", s, key[2] + 1))
+        sends += [("bz", q, -s * key[2], 1) for q in (1, -1)]
+    elif kind == "bz":
+        if key[3] < hops_bz(s, key[2]):
+            sends.append(("bz", s, key[2], key[3] + 1))
+    elif kind == "xo":
+        sends.append(("xf", s, key[2]))
+        if key[2] + 2 < ROW_CHUNKS:
+            sends.append(("xo", s, key[2] + 2))
+    return sends
+
+
+def arrival_order(left, right, row_bytes):
+    cost = {"az": left, "ay": left, "by": right, "bz": right, "xo": row_bytes, "xf": row_bytes // 2}
+    free, queue, order, count = {}, [], [], 0
+    pending = [(0.0, key) for key in first_sends()]
+    while pending or queue:
+        for now, key in pending:
+            link = ({"a": key[0][1], "b": key[0][1], "x": "x"}[key[0][0]], key[1])
+            free[link] = max(now, free.get(link, 0.0)) + cost[key[0]] / 46.5e3
+            heapq.heappush(queue, (free[link] + 1.6, count, key))
+            count += 1
+        now, _, key = heapq.heappop(queue)
+        order.append(key)
+        pending = [(now, k) for k in next_sends(key)]
+    return order
+
+
+def project_kernel(
+    order, x_ref, gain_ref, wq_ref, wk_ref, wv_ref, cos_ref, sin_ref, out_ref,
+    wa, wb, raw, normed, send_sems, recv_sems, pass_sems, passed_sems, local_sems,
+):
+    me = lax.axis_index("dp")
+    my_x = lax.axis_index("tensor")
+    my_y, my_z, my_c = me // (Z_CHIPS * CORES), (me // CORES) % Z_CHIPS, me % CORES
+    other_c = 1 - my_c
+    rows = raw.shape[1] // ROW_CHUNKS
+    features = raw.shape[2]
+    shard = wq_ref.shape[0]
+    left_w, right_w = wa.shape[1], wb.shape[1]
+
+    def device(dx=0, dy=0, dz=0, core=None):
+        y = (my_y + dy + Y_CHIPS) % Y_CHIPS
+        z = (my_z + dz + Z_CHIPS) % Z_CHIPS
+        core = my_c if core is None else core
+        return ((y * Z_CHIPS + z) * CORES + core, (my_x + dx + X_CHIPS) % X_CHIPS)
+
+    neighbours = [
+        device(dx=1), device(dx=-1), device(dy=1), device(dy=-1), device(dz=1), device(dz=-1),
+        device(core=other_c),
+    ]
+
+    def weight_rows(dy, dz, core):
+        y = (my_y + dy + 2 * Y_CHIPS) % Y_CHIPS
+        z = (my_z + dz + 2 * Z_CHIPS) % Z_CHIPS
+        return pl.ds(pl.multiple_of(((core * Y_CHIPS + y) * Z_CHIPS + z) * shard, shard), shard)
+
+    sibling = device(core=other_c)
+    names = {key: n for n, key in enumerate(order)}
+
+    def piece(key, back):
+        kind, s = key[:2]
+        if kind == "az":
+            return wa.at[weight_rows(0, -s * back, my_c), :]
+        if kind == "ay":
+            return wa.at[weight_rows(-s * back, key[2], my_c), :]
+        if kind == "by":
+            return wb.at[weight_rows(-s * back, 0, my_c), :]
+        if kind == "bz":
+            return wb.at[weight_rows(key[2], -s * back, my_c), :]
+        at = (my_x - s * back + 2 * X_CHIPS) % X_CHIPS
+        chunk = pl.ds(key[2] * rows, rows)
+        if kind == "xo":
+            return raw.at[at, chunk, :]
+        half = features // 2
+        return raw.at[at, chunk, pl.ds(0 if s == 1 else half, half)]
+
+    def made(key):
+        return {"az": key[-1] - 1, "ay": key[-1] - 1, "by": key[-1] - 1, "bz": key[-1] - 1, "xo": 0, "xf": 1}[key[0]]
+
+    def copy(key):
+        n = names[key]
+        axis = {"a": "d" + key[0][1], "b": "d" + key[0][1], "x": "dx"}[key[0][0]]
+        ref = piece(key, made(key))
+        return pltpu.make_async_remote_copy(
+            src_ref=ref, dst_ref=ref, send_sem=send_sems.at[n], recv_sem=recv_sems.at[n],
+            device_id=device(**{axis: key[1]}), device_id_type=MESH,
+        )
+
+    def landing(key):
+        n = names[key]
+        ref = piece(key, made(key) + 1)
+        return pltpu.make_async_remote_copy(
+            src_ref=ref, dst_ref=ref, send_sem=send_sems.at[n], recv_sem=recv_sems.at[n],
+            device_id=sibling, device_id_type=MESH,
+        )
+
+    passes = []
+
+    def pass_on(buffer, ref):
+        c = pltpu.make_async_remote_copy(
+            src_ref=ref, dst_ref=ref, send_sem=pass_sems.at[len(passes)], recv_sem=passed_sems.at[buffer],
+            device_id=sibling, device_id_type=MESH,
+        )
+        c.start()
+        passes.append(c)
+
+    own = weight_rows(0, 0, my_c)
+    local = [
+        pltpu.make_async_copy(wq_ref.at[:, pl.ds(0, left_w)], wa.at[own, :], local_sems.at[0]),
+        pltpu.make_async_copy(
+            wq_ref.at[:, pl.ds(left_w, right_w - 2 * LANES)],
+            wb.at[own, pl.ds(0, right_w - 2 * LANES)], local_sems.at[1],
+        ),
+        pltpu.make_async_copy(wk_ref, wb.at[own, pl.ds(right_w - 2 * LANES, LANES)], local_sems.at[2]),
+        pltpu.make_async_copy(wv_ref, wb.at[own, pl.ds(right_w - LANES, LANES)], local_sems.at[3]),
+        pltpu.make_async_copy(x_ref, raw.at[my_x], local_sems.at[4]),
+    ]
+    for c in local:
+        c.start()
+    barrier = pltpu.get_barrier_semaphore()
+    for n in neighbours:
+        pl.semaphore_signal(barrier, inc=1, device_id=n, device_id_type=MESH)
+    pl.semaphore_wait(barrier, len(neighbours))
+    for c in local:
+        c.wait()
+
+    sent = []
+
+    def send(key):
+        c = copy(key)
+        c.start()
+        sent.append(c)
+
+    for key in first_sends():
+        send(key)
+    pass_on(0, wa.at[own, :])
+    pass_on(1, wb.at[own, :])
+
+    def normalise(chunk):
+        step = 16
+
+        @pl.loop(0, rows // step)
+        def _(i):
+            at = pl.ds(pl.multiple_of(chunk * rows + i * step, step), step)
+            total = jnp.zeros((step, 1), jnp.float32)
+            for q in range(X_CHIPS):
+                v = raw[q, at, :].astype(jnp.float32)
+                total += jnp.sum(v * v, axis=1, keepdims=True)
+            scale = lax.rsqrt(total / (X_CHIPS * features) + norm_eps)
+            for q in range(X_CHIPS):
+                v = raw[q, at, :].astype(jnp.float32)
+                g = gain_ref[:, pl.ds(q * features, features)]
+                n = (v * scale * g).astype(jnp.bfloat16)
+                for z in range(Z_CHIPS):
+                    for c in range(CORES):
+                        src = (z * CORES + c) * shard
+                        dst = ((c * Y_CHIPS + q) * Z_CHIPS + z) * shard
+                        normed[at, pl.ds(dst, shard)] = n[:, src : src + shard]
+
+    halves = {}
+    for key in order:
+        landing(key).wait_recv()
+        for k in next_sends(key):
+            send(k)
+        kind = key[0]
+        if kind[0] == "a":
+            pass_on(0, piece(key, made(key) + 1))
+        elif kind[0] == "b":
+            pass_on(1, piece(key, made(key) + 1))
+        elif kind == "xf":
+            halves[key[2]] = halves.get(key[2], 0) + 1
+            if halves[key[2]] == 2:
+                normalise(key[2])
+
+    span = wa.shape[0] // CORES
+    theirs = pl.ds(pl.multiple_of(other_c * span, span), span)
+    for n, ref in enumerate((wa.at[theirs, :], wb.at[theirs, :])):
+        pltpu.make_async_remote_copy(
+            src_ref=ref, dst_ref=ref, send_sem=pass_sems.at[0], recv_sem=passed_sems.at[n],
+            device_id=sibling, device_id_type=MESH,
+        ).wait_recv()
+
+    block_rows, block = 256, 2 * LANES
+    head = HEAD_WIDTH
+    cosine, sine = cos_ref[...], sin_ref[...]
+
+    def turn(v):
+        shaped = v.reshape(block_rows // 8, 8, head)
+        turned = pltpu.roll(v, head // 2, 1).reshape(block_rows // 8, 8, head)
+        return (shaped * cosine[None] + turned * sine[None]).reshape(block_rows, head)
+
+    @pl.loop(0, normed.shape[0] // block_rows)
+    def _(m):
+        at = pl.ds(pl.multiple_of(m * block_rows, block_rows), block_rows)
+
+        def product(w, n):
+            return jnp.dot(normed[at, :], w[:, pl.ds(n, block)], preferred_element_type=jnp.float32)
+
+        def store(v, column, turned):
+            for h in range(2):
+                part = v[:, h * head : (h + 1) * head]
+                part = turn(part) if turned[h] else part
+                out_ref[at, pl.ds(column + h * head, head)] = part.astype(jnp.bfloat16)
+
+        @pl.loop(0, left_w // block)
+        def _(n):
+            col = pl.multiple_of(n * block, block)
+            store(product(wa, col), col, (True, True))
+
+        store(product(wb, 0), left_w, (True, True))
+        store(product(wb, block), left_w + block, (True, False))
+
+    for c in sent + passes:
+        c.wait_send()
+
+
+def project(activations, norm_gain, w_query, w_key, w_value, cosine, sine):
+    rows, features = activations.shape
+    shard = w_query.shape[0]
+    columns = w_query.shape[1] + w_key.shape[1] + w_value.shape[1]
+    right = columns - LEFT_COLUMNS
+    depth = shard * Y_CHIPS * Z_CHIPS * CORES
+    order = arrival_order(shard * LEFT_COLUMNS * 2, shard * right * 2, rows // ROW_CHUNKS * features * 2)
+    passes = 2 * Y_CHIPS * Z_CHIPS
+    vmem = pl.BlockSpec(memory_space=pltpu.VMEM)
+    hbm = pl.BlockSpec(memory_space=pl.ANY)
+    return pl.pallas_call(
+        functools.partial(project_kernel, order),
+        out_shape=jax.ShapeDtypeStruct((rows, columns), jnp.bfloat16),
+        in_specs=[hbm, vmem, hbm, hbm, hbm, vmem, vmem],
+        out_specs=vmem,
+        scratch_shapes=[
+            pltpu.VMEM((depth, LEFT_COLUMNS), jnp.bfloat16),
+            pltpu.VMEM((depth, right), jnp.bfloat16),
+            pltpu.VMEM((X_CHIPS, rows, features), jnp.bfloat16),
+            pltpu.VMEM((rows, X_CHIPS * features), jnp.bfloat16),
+            pltpu.SemaphoreType.DMA((len(order),)),
+            pltpu.SemaphoreType.DMA((len(order),)),
+            pltpu.SemaphoreType.DMA((passes,)),
+            pltpu.SemaphoreType.DMA((2,)),
+            pltpu.SemaphoreType.DMA((5,)),
+        ],
+        compiler_params=pltpu.CompilerParams(
+            collective_id=0, has_side_effects=True, vmem_limit_bytes=60 * 1024 * 1024
+        ),
+        name="project",
+    )(activations, norm_gain.reshape(1, -1), w_query, w_key, w_value, cosine, sine)
+
+
+def rotation_tables(positions, head_dim):
+    half_width = head_dim // 2
     steps_range = jnp.arange(half_width, dtype=jnp.float32)
-    frequency = jnp.exp(steps_range * (-2.0 * math.log(rope_base) / vectors.shape[-1]))
-    angles = token_positions[..., None, None] * frequency
-    cosine = jnp.cos(angles)
-    sine_table = jnp.sin(angles)
-    first_half = vectors[..., :half_width]
-    second_half = vectors[..., half_width:]
-    return jnp.concatenate(
-        [
-            first_half * cosine - second_half * sine_table,
-            second_half * cosine + first_half * sine_table,
-        ],
-        axis=-1,
-    )
-
-
-def project(source_rows, norm_gain, w_query, w_key, w_value):
-    packed_weight = jnp.concatenate([w_query, w_key, w_value], axis=1)
-    weight = lax.all_gather(packed_weight, "dp", axis=0, tiled=True)
-    gathered = lax.all_gather(source_rows, "tensor", axis=1, tiled=True)
-    widened = gathered.astype(jnp.float32)
-    row_scale = lax.rsqrt(jnp.mean(widened * widened, axis=1, keepdims=True) + norm_eps)
-    normed = (widened * row_scale * norm_gain).astype(jnp.bfloat16)
-    return jnp.dot(normed, weight, preferred_element_type=jnp.float32)
-
-
-def rotate_round(projected, token_positions, rotated_width, head_dim):
-    total_rows = projected.shape[0]
-    rotated = rotary_embedding(
-        projected[:, :rotated_width].reshape(total_rows, -1, head_dim), token_positions
-    ).reshape(total_rows, -1)
-    return jnp.concatenate([rotated, projected[:, rotated_width:]], axis=1).astype(jnp.bfloat16)
+    frequency = jnp.exp(steps_range * (-2.0 * math.log(rope_base) / head_dim))
+    angles = positions[:, None] * frequency
+    cosine, sine = jnp.cos(angles), jnp.sin(angles)
+    return jnp.concatenate([cosine, cosine], axis=1), jnp.concatenate([-sine, sine], axis=1)
 
 
 def attend(packed, doc_lengths, query_width, key_width, head_dim, doc_max):
@@ -113,11 +381,9 @@
     send_index = (
         holder_grid[:, None, :] * rows_peer + jnp.arange(rows_peer)[None, :, None]
     ).reshape(-1)
-    token_positions = (
-        my_shard + shard_count * (jnp.arange(token_rows) % rows_peer)
-    ).astype(jnp.float32)
-    projected = project(activations, norm_gain, w_query, w_key, w_value)
-    packed = rotate_round(projected, token_positions, query_width + key_width, head_dim)
+    positions = (my_shard + shard_count * (jnp.arange(8) % rows_peer)).astype(jnp.float32)
+    cosine, sine = rotation_tables(positions, head_dim)
+    packed = project(activations, norm_gain, w_query, w_key, w_value, cosine, sine)
     outgoing = jnp.take(packed, send_index, axis=0, mode="clip").reshape(
         docs_here, rows_peer, shard_count, -1
     )

time: 293 us -> 154 us (0.53)
  waiting for transfers between devices: 231 us -> 33.1 us
  Pallas kernels: 0 us -> 95.1 us
  matrix products: 18.6 us -> 2.07 us
  between operations: 13.6 us -> 0.18 us
  other arithmetic: 12 us -> 4.96 us
  starting transfers between devices: 6.01 us -> 9.4 us
    all_gather x2 -> x0, waiting for transfers between devices: 197 us -> none  [the longest x1 109 us: project(): weight = lax.all_gather(packed_weight, 'dp', axis=0, tiled=True)]
    pallas_call x0 -> x1, Pallas kernels: none -> 95.1 us  [project(): pl.pallas_call(functools.partial(project_kernel, order), out_shape=jax.Sh...]
    dot_general x1 -> x0, matrix products: 16.5 us -> none  [project(): return jnp.dot(normed, weight, preferred_element_type=jnp.float32)]
    reduce_sum x1 -> x0, other arithmetic: 5.1 us -> none  [project(): jnp.mean(widened * widened, axis=1, keepdims=True) + norm_eps]
    slice x3 -> x0, local copies, waits for them, and re-layouts: 3.62 us -> none  [the longest x2 3.6 us: rotate_round(): projected[:, :rotated_width].reshape(total_rows, -1, head_dim)]
    all_to_all x1, starting transfers between devices: 5.97 us -> 9.4 us  [local(): lax.all_to_all(outgoing, 'dp', split_axis=2, concat_axis=2, tiled=True)]
  transfers between devices with their start and end apart: 3 -> 1, of which waited for: 3 -> 1; matrix products, arithmetic and copies ran while one was open for 3% -> 1% of each run, Pallas kernels for 0% -> 0%
where the time goes in v2:
time: 154 us
  Pallas kernels  95.1 us (62%)
  waiting for transfers between devices  33.1 us (21%)
  starting transfers between devices  9.4 us (6%)
  local copies, waits for them, and re-layouts  9.04 us (6%)
  other arithmetic  4.96 us (3%)
  matrix products  2.07 us (1%)
    pallas_call x1, Pallas kernels, project(): pl.pallas_call(functools.partial(project_kernel, order), out_shape=jax.Sh...  95.1 us
    all_to_all x1, waiting for transfers between devices, local(): lax.all_to_all(outgoing, 'dp', split_axis=2, concat_axis=2, tiled=True)  33.1 us
    all_to_all x1, starting transfers between devices, local(): lax.all_to_all(outgoing, 'dp', split_axis=2, concat_axis=2, tiled=True)  9.4 us
    gather x1, local copies, waits for them, and re-layouts, local(): jnp.take(packed, send_index, axis=0, mode='clip')  4.6 us
  transfers between devices with their start and end apart: 1, of which 1 were waited for; matrix products, arithmetic and copies ran while one was open for 1% of the time, Pallas kernels for 0%

profile of v2, /device:TPU:1, one launch (start us, length us, event | category | flops | bytes accessed | tf_op | source)
XLA Modules:
  0.0 153.9 jit_solution(4671998816136123999)
XLA Ops:
  0.0 0.9 convert_reduce_fusion
  0.9 0.7 multiply_add_fusion
  1.6 0.1 select_reduce_fusion
  1.7 0.1 mul.63
  1.9 0.1 copy.24
  1.9 0.1 reshape.143
  2.0 0.1 fusion.12
  2.2 0.7 pad_maximum_fusion
  2.8 95.1 %project.1 = bf16[512,1280]{1,0:T(8,128)(2,1)} custom-call(bf16[512,2048]{1,0:T(8,128)(2,1)} %x_ref.1, f32[1,8192]{1,0:T(1,128)} %bitcast.59, bf16[128,1024]{1,0:T(8,128)(2,1)} %wq_ref.1, bf16[128,128]{1,0:T(8,128)(2,1)} %wk_ref.1, bf16[128,128]{1,0:T(8,128)(2,1)} %wv_ref.1, f32[8,128]{1,0:T(8,128)} %get-tuple-element.12.cos_ref, ...), custom_call_target="tpu_custom_call" | custom-call | tf_op jit(solution)/shard_map/project/pallas_call | solution.py:287
  98.0 4.6 %gather_fusion.1 = bf16[512,1280]{1,0:T(8,128)(2,1)S(1)} fusion(bf16[512,1280]{1,0:T(8,128)(2,1)} %project.1, s32[1024]{0:T(1024)S(1)} %pad_clamp_fusion), kind=kCustom, calls=%fused_computation.1 | custom fusion | bytes 2623488 | tf_op jit(solution)/shard_map/jit(_take)/gather | solution.py:387
  102.6 0.0 copy-start
  102.6 0.0 copy-start.1
  102.6 0.0 copy-start.2
  102.6 2.1 %copy.25 = bf16[2,4,64,1280]{3,1,0,2:T(4,128)(2,1)} copy(bf16[2,4,64,1280]{3,2,1,0:T(8,128)(2,1)S(1)} %bitcast.51) | data formatting | bytes 2621440 | tf_op jit(solution)/shard_map/reshape | solution.py:387
  104.7 9.4 %all-to-all-start = ((bf16[2,4,64,1280]{3,1,0,2:T(4,128)(2,1)}), bf16[2,4,64,1280]{3,1,0,2:T(4,128)(2,1)S(1)}, u32[]{:S(2)}, u32[]{:S(2)}) async-start(bf16[2,4,64,1280]{3,1,0,2:T(4,128)(2,1)} %copy.25), calls=%async_computation | async-start | bytes 2621440 | tf_op jit(solution)/shard_map/all_to_all | solution.py:390
  114.1 0.0 copy-done
  114.1 0.0 copy-done.1
  114.1 0.1 select_reduce_fusion.1
  114.2 0.0 copy-done.2
  114.2 0.1 compare_select_fusion
  114.3 0.6 gather_fusion
  115.0 0.1 and_select_fusion.1
  115.0 0.1 iota_compare_fusion.4
  115.2 33.1 %all-to-all-done = bf16[2,4,64,1280]{3,1,0,2:T(4,128)(2,1)S(1)} async-done(((bf16[2,4,64,1280]{3,1,0,2:T(4,128)(2,1)}), bf16[2,4,64,1280]{3,1,0,2:T(4,128)(2,1)S(1)}, u32[]{:S(2)}, u32[]{:S(2)}) %all-to-all-start) | async-done | bytes 1310752 | tf_op jit(solution)/shard_map/all_to_all | solution.py:390
  148.3 0.2 copy.26
  148.5 0.1 slice_bitcast_fusion
  148.6 0.3 copy.36
  148.9 0.8 fusion.1
  149.7 0.9 fusion
  150.6 1.3 fusion.6
  151.9 0.8 copy.30
  152.6 1.2 fusion.2
  (10 shorter events, 0.1 us)
Async XLA Ops:
  102.6 11.5 %copy-start = (s32[30]{0:T(128)S(1)}, s32[30]{0:T(128)}, u32[]{:S(2)}) copy-start(s32[30]{0:T(128)} %param.16) | copy-start | bytes 364
  102.6 11.5 %copy-start.1 = (s32[128]{0:T(128)S(1)}, s32[128]{0:T(128)}, u32[]{:S(2)}) copy-start(s32[128]{0:T(128)} %param.15) | copy-start | bytes 1540
  102.6 11.6 %copy-start.2 = (s32[128]{0:T(128)S(1)}, s32[128]{0:T(128)}, u32[]{:S(2)}) copy-start(s32[128]{0:T(128)} %param.14) | copy-start | bytes 1540
  104.7 43.5 %all-to-all-start = ((bf16[2,4,64,1280]{3,1,0,2:T(4,128)(2,1)}), bf16[2,4,64,1280]{3,1,0,2:T(4,128)(2,1)S(1)}, u32[]{:S(2)}, u32[]{:S(2)}) async-start(bf16[2,4,64,1280]{3,1,0,2:T(4,128)(2,1)} %copy.25), calls=%async_computation | async-start | bytes 2621440 | tf_op jit(solution)/shard_map/all_to_all | solution.py:390

commit v3 on v2

--- a/solution.py
+++ b/solution.py
@@ -20,6 +20,8 @@
 LANES = 128
 Y_CHIPS, Z_CHIPS, CORES, X_CHIPS = 4, 8, 2, 4
 ROW_CHUNKS = 4
+CHUNK_DY = (2, 1, 3, 0)
+SEND_DZ = (4, 3, 5, 2, 6, 1, 7, 0)
 LEFT_COLUMNS = 768
 
 
@@ -41,8 +43,11 @@
 
 def first_sends():
     sends = [("az", s, 1) for s in (1, -1)] + [("by", s, 1) for s in (1, -1)]
-    sends += [("ay", s, 0, 1) for s in (1, -1)] + [("bz", s, 0, 1) for s in (1, -1)]
-    return sends + [("xo", s, r) for r in range(2) for s in (1, -1)]
+    return sends + [("ay", s, 0, 1) for s in (1, -1)] + [("bz", s, 0, 1) for s in (1, -1)]
+
+
+def first_rows(chunk):
+    return [("xo", s, chunk) for s in (1, -1)]
 
 
 def next_sends(key):
@@ -72,7 +77,7 @@
 def arrival_order(left, right, row_bytes):
     cost = {"az": left, "ay": left, "by": right, "bz": right, "xo": row_bytes, "xf": row_bytes // 2}
     free, queue, order, count = {}, [], [], 0
-    pending = [(0.0, key) for key in first_sends()]
+    pending = [(0.0, key) for key in first_sends() + first_rows(0) + first_rows(1)]
     while pending or queue:
         for now, key in pending:
             link = ({"a": key[0][1], "b": key[0][1], "x": "x"}[key[0][0]], key[1])
@@ -86,8 +91,9 @@
 
 
 def project_kernel(
-    order, x_ref, gain_ref, wq_ref, wk_ref, wv_ref, cos_ref, sin_ref, out_ref,
-    wa, wb, raw, normed, send_sems, recv_sems, pass_sems, passed_sems, local_sems,
+    order, x_ref, place_ref, gain_ref, wq_ref, wk_ref, wv_ref, cos_ref, sin_ref, arrived,
+    wa, wb, mine, raw, normed, packed,
+    send_sems, recv_sems, pass_sems, passed_sems, local_sems, out_sems, in_sem,
 ):
     me = lax.axis_index("dp")
     my_x = lax.axis_index("tensor")
@@ -173,7 +179,7 @@
         ),
         pltpu.make_async_copy(wk_ref, wb.at[own, pl.ds(right_w - 2 * LANES, LANES)], local_sems.at[2]),
         pltpu.make_async_copy(wv_ref, wb.at[own, pl.ds(right_w - LANES, LANES)], local_sems.at[3]),
-        pltpu.make_async_copy(x_ref, raw.at[my_x], local_sems.at[4]),
+        pltpu.make_async_copy(x_ref, mine, local_sems.at[4]),
     ]
     for c in local:
         c.start()
@@ -181,7 +187,7 @@
     for n in neighbours:
         pl.semaphore_signal(barrier, inc=1, device_id=n, device_id_type=MESH)
     pl.semaphore_wait(barrier, len(neighbours))
-    for c in local:
+    for c in local[:4]:
         c.wait()
 
     sent = []
@@ -195,6 +201,25 @@
         send(key)
     pass_on(0, wa.at[own, :])
     pass_on(1, wb.at[own, :])
+
+    def order_rows(chunk):
+        p = lax.broadcasted_iota(jnp.int32, (rows, raw.shape[1]), 0)
+        y = (my_y + CHUNK_DY[chunk]) % Y_CHIPS
+        z = (my_z + (p >> 4)) & (Z_CHIPS - 1)
+        c = (my_c + (p >> 3)) & (CORES - 1)
+        wanted = ((y * Z_CHIPS + z) * CORES + c) * 8 + (p & 7)
+        pick = jnp.where(wanted == place_ref[...], 1.0, 0.0).astype(jnp.bfloat16)
+        width = 512
+        for n in range(0, features, width):
+            picked = jnp.dot(pick, mine[:, pl.ds(n, width)], preferred_element_type=jnp.float32)
+            raw[my_x, pl.ds(chunk * rows, rows), pl.ds(n, width)] = picked.astype(jnp.bfloat16)
+
+    local[4].wait()
+    for chunk in range(ROW_CHUNKS):
+        order_rows(chunk)
+        if chunk < 2:
+            for key in first_rows(chunk):
+                send(key)
 
     def normalise(chunk):
         step = 16
@@ -217,7 +242,58 @@
                         dst = ((c * Y_CHIPS + q) * Z_CHIPS + z) * shard
                         normed[at, pl.ds(dst, shard)] = n[:, src : src + shard]
 
+    block_rows, block = 2 * rows, 2 * LANES
+    head = HEAD_WIDTH
+    cosine, sine = cos_ref[...], sin_ref[...]
+
+    def turn(v):
+        turned = pltpu.roll(v, head // 2, 1).reshape(block_rows // 8, 8, head)
+        return v.reshape(block_rows // 8, 8, head) * cosine[None] + turned * sine[None]
+
+    def multiply(m):
+        at = pl.ds(m * block_rows, block_rows)
+        groups = pl.ds(m * block_rows // 8, block_rows // 8)
+
+        def product(w, n):
+            return jnp.dot(normed[at, :], w[:, pl.ds(n, block)], preferred_element_type=jnp.float32)
+
+        def store(v, column, turned):
+            for h in range(2):
+                part = v[:, h * head : (h + 1) * head]
+                part = turn(part) if turned[h] else part.reshape(block_rows // 8, 8, head)
+                packed[groups, :, pl.ds(column + h * head, head)] = part.astype(jnp.bfloat16)
+
+        @pl.loop(0, left_w // block)
+        def _(n):
+            col = pl.multiple_of(n * block, block)
+            store(product(wa, col), col, (True, True))
+
+        store(product(wb, 0), left_w, (True, True))
+        store(product(wb, block), left_w + block, (True, False))
+
+    outgoing = []
+
+    def hand_out(chunk):
+        for dz in SEND_DZ:
+            for dc in range(CORES):
+                group = (chunk * Z_CHIPS + dz) * CORES + dc
+                core = other_c if dc else my_c
+                if CHUNK_DY[chunk] or dz or dc:
+                    c = pltpu.make_async_remote_copy(
+                        src_ref=packed.at[group], dst_ref=arrived.at[me], send_sem=out_sems.at[group], recv_sem=in_sem,
+                        device_id=device(dy=CHUNK_DY[chunk], dz=dz, core=core), device_id_type=MESH,
+                    )
+                    outgoing.append(c)
+                else:
+                    c = pltpu.make_async_copy(packed.at[group], arrived.at[me], out_sems.at[group])
+                    own_group.append(c)
+                c.start()
+
+    own_group = []
     halves = {}
+    left = sum(key[0][0] != "x" for key in order)
+    span = wa.shape[0] // CORES
+    theirs = pl.ds(pl.multiple_of(other_c * span, span), span)
     for key in order:
         landing(key).wait_recv()
         for k in next_sends(key):
@@ -231,50 +307,32 @@
             halves[key[2]] = halves.get(key[2], 0) + 1
             if halves[key[2]] == 2:
                 normalise(key[2])
-
-    span = wa.shape[0] // CORES
-    theirs = pl.ds(pl.multiple_of(other_c * span, span), span)
-    for n, ref in enumerate((wa.at[theirs, :], wb.at[theirs, :])):
-        pltpu.make_async_remote_copy(
-            src_ref=ref, dst_ref=ref, send_sem=pass_sems.at[0], recv_sem=passed_sems.at[n],
-            device_id=sibling, device_id_type=MESH,
-        ).wait_recv()
-
-    block_rows, block = 256, 2 * LANES
-    head = HEAD_WIDTH
-    cosine, sine = cos_ref[...], sin_ref[...]
-
-    def turn(v):
-        shaped = v.reshape(block_rows // 8, 8, head)
-        turned = pltpu.roll(v, head // 2, 1).reshape(block_rows // 8, 8, head)
-        return (shaped * cosine[None] + turned * sine[None]).reshape(block_rows, head)
-
-    @pl.loop(0, normed.shape[0] // block_rows)
-    def _(m):
-        at = pl.ds(pl.multiple_of(m * block_rows, block_rows), block_rows)
-
-        def product(w, n):
-            return jnp.dot(normed[at, :], w[:, pl.ds(n, block)], preferred_element_type=jnp.float32)
-
-        def store(v, column, turned):
-            for h in range(2):
-                part = v[:, h * head : (h + 1) * head]
-                part = turn(part) if turned[h] else part
-                out_ref[at, pl.ds(column + h * head, head)] = part.astype(jnp.bfloat16)
-
-        @pl.loop(0, left_w // block)
-        def _(n):
-            col = pl.multiple_of(n * block, block)
-            store(product(wa, col), col, (True, True))
-
-        store(product(wb, 0), left_w, (True, True))
-        store(product(wb, block), left_w + block, (True, False))
-
-    for c in sent + passes:
+        left -= kind[0] != "x"
+        if kind[0] != "x" and left == 0:
+            for n, ref in enumerate((wa.at[theirs, :], wb.at[theirs, :])):
+                pltpu.make_async_remote_copy(
+                    src_ref=ref, dst_ref=ref, send_sem=pass_sems.at[0], recv_sem=passed_sems.at[n],
+                    device_id=sibling, device_id_type=MESH,
+                ).wait_recv()
+            assert halves[0] == halves[1] == 2
+            multiply(0)
+            hand_out(0)
+            hand_out(1)
+    multiply(1)
+    hand_out(2)
+    hand_out(3)
+
+    for c in sent + passes + outgoing:
         c.wait_send()
-
-
-def project(activations, norm_gain, w_query, w_key, w_value, cosine, sine):
+    own_group[0].wait()
+    groups = arrived.at[pl.ds(0, len(outgoing))]
+    pltpu.make_async_remote_copy(
+        src_ref=groups, dst_ref=groups, send_sem=out_sems.at[0], recv_sem=in_sem,
+        device_id=sibling, device_id_type=MESH,
+    ).wait_recv()
+
+
+def project(activations, place, norm_gain, w_query, w_key, w_value, cosine, sine):
     rows, features = activations.shape
     shard = w_query.shape[0]
     columns = w_query.shape[1] + w_key.shape[1] + w_value.shape[1]
@@ -286,25 +344,29 @@
     hbm = pl.BlockSpec(memory_space=pl.ANY)
     return pl.pallas_call(
         functools.partial(project_kernel, order),
-        out_shape=jax.ShapeDtypeStruct((rows, columns), jnp.bfloat16),
-        in_specs=[hbm, vmem, hbm, hbm, hbm, vmem, vmem],
-        out_specs=vmem,
+        out_shape=jax.ShapeDtypeStruct((rows // 8, 8, columns), jnp.bfloat16),
+        in_specs=[hbm, vmem, vmem, hbm, hbm, hbm, vmem, vmem],
+        out_specs=hbm,
         scratch_shapes=[
             pltpu.VMEM((depth, LEFT_COLUMNS), jnp.bfloat16),
             pltpu.VMEM((depth, right), jnp.bfloat16),
+            pltpu.VMEM((rows, features), jnp.bfloat16),
             pltpu.VMEM((X_CHIPS, rows, features), jnp.bfloat16),
             pltpu.VMEM((rows, X_CHIPS * features), jnp.bfloat16),
+            pltpu.VMEM((rows // 8, 8, columns), jnp.bfloat16),
             pltpu.SemaphoreType.DMA((len(order),)),
             pltpu.SemaphoreType.DMA((len(order),)),
             pltpu.SemaphoreType.DMA((passes,)),
             pltpu.SemaphoreType.DMA((2,)),
             pltpu.SemaphoreType.DMA((5,)),
+            pltpu.SemaphoreType.DMA((rows // 8,)),
+            pltpu.SemaphoreType.DMA,
         ],
         compiler_params=pltpu.CompilerParams(
             collective_id=0, has_side_effects=True, vmem_limit_bytes=60 * 1024 * 1024
         ),
         name="project",
-    )(activations, norm_gain.reshape(1, -1), w_query, w_key, w_value, cosine, sine)
+    )(activations, place, norm_gain.reshape(1, -1), w_query, w_key, w_value, cosine, sine)
 
 
 def rotation_tables(positions, head_dim):
@@ -316,36 +378,47 @@
     return jnp.concatenate([cosine, cosine], axis=1), jnp.concatenate([-sine, sine], axis=1)
 
 
-def attend(packed, doc_lengths, query_width, key_width, head_dim, doc_max):
-    total_rows = packed.shape[0]
-    doc_total = total_rows // doc_max
-    value_head_rows = key_width // head_dim
-    heads_per_group = query_width // key_width
-    queries = packed[:, :query_width].reshape(
-        doc_total, doc_max, value_head_rows, heads_per_group, head_dim
-    )
-    key_rows = packed[:, query_width : query_width + key_width].reshape(
-        doc_total, doc_max, value_head_rows, head_dim
-    )
-    value_rows = packed[:, query_width + key_width :].reshape(
-        doc_total, doc_max, value_head_rows, head_dim
-    )
-    scores = jnp.einsum(
-        "jqhgd,jkhd->jhgqk", queries, key_rows, preferred_element_type=jnp.float32
-    ) / math.sqrt(head_dim)
-    order_range = jnp.arange(doc_max)
-    causal = order_range[:, None] >= order_range[None, :]
-    scores = jnp.where(causal, scores, -jnp.inf)
-    row_peak = jnp.max(scores, axis=-1, keepdims=True)
-    exponent = jnp.exp(scores - row_peak)
-    probability = (exponent / jnp.sum(exponent, axis=-1, keepdims=True)).astype(jnp.bfloat16)
-    blended = jnp.einsum(
-        "jhgqk,jkhd->jqhgd", probability, value_rows, preferred_element_type=jnp.float32
-    )
-    blended = blended.reshape(doc_total, doc_max, query_width)
-    row_valid = order_range[None, :] < doc_lengths[:, None]
-    result = jnp.where(row_valid[..., None], blended, 0.0)
-    return result.reshape(total_rows, query_width).astype(jnp.bfloat16)
+def attend_kernel(lengths_ref, rows_ref, out_ref, ordered, *, query_width, head, docs):
+    total = rows_ref.shape[0]
+    doc_rows = total // docs
+    shards = total // 8
+    per_doc = 8 // docs
+    s = lax.broadcasted_iota(jnp.int32, (total, total), 0)
+    i = lax.broadcasted_iota(jnp.int32, (total, total), 1)
+    source = (s % shards) * 8 + (s // doc_rows) * per_doc + (s // shards) % per_doc
+    pick = jnp.where(i == source, 1.0, 0.0).astype(jnp.bfloat16)
+    ordered[...] = jnp.dot(pick, rows_ref[...], preferred_element_type=jnp.float32).astype(jnp.bfloat16)
+    a = lax.broadcasted_iota(jnp.int32, (doc_rows, doc_rows), 0)
+    b = lax.broadcasted_iota(jnp.int32, (doc_rows, doc_rows), 1)
+    t = lax.broadcasted_iota(jnp.int32, (doc_rows, head), 0)
+    for doc in range(docs):
+        at = pl.ds(doc * doc_rows, doc_rows)
+        key = ordered[at, pl.ds(query_width, head)]
+        value = ordered[at, pl.ds(query_width + head, head)]
+        kept = t < lengths_ref[doc]
+        for n in range(query_width // head):
+            query = ordered[at, pl.ds(n * head, head)]
+            score = lax.dot_general(
+                query, key, (((1,), (1,)), ((), ())), preferred_element_type=jnp.float32
+            ) / math.sqrt(head)
+            score = jnp.where(a >= b, score, -jnp.inf)
+            exponent = jnp.exp(score - jnp.max(score, axis=1, keepdims=True))
+            probs = (exponent / jnp.sum(exponent, axis=1, keepdims=True)).astype(jnp.bfloat16)
+            blended = jnp.dot(probs, value, preferred_element_type=jnp.float32)
+            out_ref[at, pl.ds(n * head, head)] = jnp.where(kept, blended, 0.0).astype(jnp.bfloat16)
+
+
+def attend(rows, doc_lengths, query_width, head):
+    total, columns = rows.shape
+    vmem = pl.BlockSpec(memory_space=pltpu.VMEM)
+    return pl.pallas_call(
+        functools.partial(attend_kernel, query_width=query_width, head=head, docs=doc_lengths.shape[0]),
+        out_shape=jax.ShapeDtypeStruct((total, query_width), jnp.bfloat16),
+        in_specs=[pl.BlockSpec(memory_space=pltpu.SMEM), vmem],
+        out_specs=vmem,
+        scratch_shapes=[pltpu.VMEM((total, columns), jnp.bfloat16)],
+        name="attend",
+    )(doc_lengths, rows)
 
 
 def local(
@@ -356,40 +429,24 @@
     doc_count = lengths.shape[0]
     token_rows = activations.shape[0]
     rows_peer = token_rows // doc_count
-    doc_max = rows_peer * shard_count
     docs_here = doc_count // shard_count
-    head_dim = HEAD_WIDTH
     query_width = w_query.shape[1]
-    key_width = w_key.shape[1]
+    doc_order = jnp.arange(doc_count)
+    earlier = (dest_shard[:, None] == dest_shard[None, :]) & (doc_order[:, None] < doc_order[None, :])
+    doc_rank = jnp.sum(earlier.astype(jnp.int32), axis=0)
+    slot = dest_shard * docs_here + doc_rank
+    place = (slot[:, None] * rows_peer + jnp.arange(rows_peer)[None, :]).reshape(1, -1)
     language_table = jnp.arange(lang_caps.shape[0])
     cap_of_doc = jnp.sum(
-        jnp.where(languages[:, None] == language_table[None, :], lang_caps[None, :], 0), axis=1
+        jnp.where(languages[None, :] == language_table[:, None], lang_caps[:, None], 0), axis=0
     )
     capped = jnp.minimum(lengths, cap_of_doc)
-    doc_order = jnp.arange(doc_count)
-    same_dest = dest_shard[:, None] == dest_shard[None, :]
-    doc_rank = jnp.sum(
-        (same_dest & (doc_order[None, :] < doc_order[:, None])).astype(jnp.int32), axis=1
-    )
-    target_slot = dest_shard * docs_here + doc_rank
-    holder = jnp.sum(
-        jnp.where(doc_order[:, None] == target_slot[None, :], doc_order[None, :], 0), axis=1
-    )
-    mine = lax.dynamic_slice_in_dim(holder, my_shard * docs_here, docs_here)
-    doc_lengths = jnp.take(capped, mine)
-    holder_grid = jnp.transpose(holder.reshape(shard_count, docs_here))
-    send_index = (
-        holder_grid[:, None, :] * rows_peer + jnp.arange(rows_peer)[None, :, None]
-    ).reshape(-1)
+    mine = my_shard * docs_here + jnp.arange(docs_here)
+    doc_lengths = jnp.sum(jnp.where(slot[None, :] == mine[:, None], capped[None, :], 0), axis=1)
     positions = (my_shard + shard_count * (jnp.arange(8) % rows_peer)).astype(jnp.float32)
-    cosine, sine = rotation_tables(positions, head_dim)
-    packed = project(activations, norm_gain, w_query, w_key, w_value, cosine, sine)
-    outgoing = jnp.take(packed, send_index, axis=0, mode="clip").reshape(
-        docs_here, rows_peer, shard_count, -1
-    )
-    arrived = lax.all_to_all(outgoing, "dp", split_axis=2, concat_axis=2, tiled=True)
-    moved_rows = arrived.reshape(docs_here * doc_max, -1)
-    return attend(moved_rows, doc_lengths, query_width, key_width, head_dim, doc_max)
+    cosine, sine = rotation_tables(positions, HEAD_WIDTH)
+    arrived = project(activations, place, norm_gain, w_query, w_key, w_value, cosine, sine)
+    return attend(arrived.reshape(token_rows, -1), doc_lengths, query_width, HEAD_WIDTH)
 
 
 def solution(mesh):

time: 154 us -> 122 us (0.79)
  waiting for transfers between devices: 33.1 us -> 0 us
  Pallas kernels: 95.1 us -> 116 us
  starting transfers between devices: 9.4 us -> 0 us
  local copies, waits for them, and re-layouts: 9.04 us -> 0.69 us
  matrix products: 2.07 us -> 0 us
    all_to_all x1 -> x0, waiting for transfers between devices: 33.1 us -> none  [local(): lax.all_to_all(outgoing, 'dp', split_axis=2, concat_axis=2, tiled=True)]
    pallas_call x1, Pallas kernels: 95.1 us -> 111 us  [project(): pl.pallas_call(functools.partial(project_kernel, order), out_shape=jax.Sh...]
    all_to_all x1 -> x0, starting transfers between devices: 9.4 us -> none  [local(): lax.all_to_all(outgoing, 'dp', split_axis=2, concat_axis=2, tiled=True)]
    pallas_call x0 -> x1, Pallas kernels: none -> 5.83 us  [attend(): pl.pallas_call(functools.partial(attend_kernel, query_width=query_width,...]
    gather x2 -> x0, local copies, waits for them, and re-layouts: 5.24 us -> none  [the longest x1 4.6 us: local(): jnp.take(packed, send_index, axis=0, mode='clip')]
    reshape x1 -> x0, local copies, waits for them, and re-layouts: 2.08 us -> none  [local(): jnp.take(packed, send_index, axis=0, mode='clip')]
    dot_general x2 -> x0, matrix products: 2.07 us -> none  [the longest x1 1.29 us: attend(): jnp.einsum('jhgqk,jkhd->jqhgd', probability, value_rows, preferred_elemen...]
  transfers between devices with their start and end apart: 1 -> 0, of which waited for: 1 -> 0; matrix products, arithmetic and copies ran while one was open for 1% -> 0% of each run, Pallas kernels for 0% -> 0%
where the time goes in v3:
time: 122 us
  Pallas kernels  116 us (95%)
  other arithmetic  4.55 us (4%)
    pallas_call x1, Pallas kernels, project(): pl.pallas_call(functools.partial(project_kernel, order), out_shape=jax.Sh...  111 us
    pallas_call x1, Pallas kernels, attend(): pl.pallas_call(functools.partial(attend_kernel, query_width=query_width,...  5.83 us

profile of v3, /device:TPU:1, one launch (start us, length us, event | category | flops | bytes accessed | tf_op | source)
XLA Modules:
  0.0 121.7 jit_solution(5117209213585964355)
XLA Ops:
  0.0 0.8 select_reduce_fusion
  0.8 0.7 min.3
  1.4 0.8 convert_reduce_fusion
  2.3 0.7 broadcast_multiply_fusion
  2.9 0.8 fusion.1.lengths_ref
  3.7 0.1 fusion.2
  3.8 0.7 pad_maximum_fusion
  4.5 0.1 iota_add_fusion
  4.6 0.7 add.62.place_ref
  5.3 110.6 %project.1 = bf16[64,8,1280]{2,1,0:T(8,128)(2,1)} custom-call(bf16[512,2048]{1,0:T(8,128)(2,1)} %x_ref.1, s32[1,512]{1,0:T(1,128)} %add.62.place_ref, f32[1,8192]{1,0:T(1,128)} %bitcast.3, bf16[128,1024]{1,0:T(8,128)(2,1)} %wq_ref.1, bf16[128,128]{1,0:T(8,128)(2,1)} %wk_ref.1, bf16[128,128]{1,0:T(8,128)(2,1)} %wv_ref.1, f32[8,128]{1,0:T(8,128)} %get-tuple-element.10.cos_ref, ...), custom_call_target="tpu_custom_call" | custom-call | tf_op jit(solution)/shard_map/project/pallas_call | solution.py:345
  115.9 5.8 %attend.1 = bf16[512,1024]{1,0:T(8,128)(2,1)} custom-call(s32[2]{0:T(128)} %fusion.1.lengths_ref, bf16[512,1280]{1,0:T(8,128)(2,1)} %bitcast.2), custom_call_target="tpu_custom_call" | custom-call | tf_op jit(solution)/shard_map/attend/pallas_call | solution.py:414
  (3 shorter events, 0.0 us)
